TPU v7x, 32 devices: a whole 2x2x4 slice. The times are simulated.
32 devices in a mesh: fsdp: 2 (over x), ctx: 16 (over z, y, core).
Axes of the slice: x: 2, y: 2, z: 4, core: 2. Of those that a mesh axis runs over, the one named last changes fastest.
Arguments:
- inputs: bfloat16 [2, 2048, 960], P('fsdp', 'ctx'), may hold values from -6 to 6
- grad_output: bfloat16 [2, 2048, 960], P('fsdp', 'ctx'), may hold values from -6 to 6
- w_query: bfloat16 [960, 960], P('fsdp', 'ctx'), may hold values from -50 to 50
- w_key: bfloat16 [960, 320], P('fsdp', 'ctx'), may hold values from -50 to 50
- w_value: bfloat16 [960, 320], P('fsdp', 'ctx'), may hold values from -0.1875 to 0.1875
- w_out: bfloat16 [960, 960], P('fsdp', 'ctx'), may hold values from -0.75 to 0.75
- w_gate: bfloat16 [960, 2560], P('fsdp', 'ctx'), may hold values from -0.1875 to 0.1875
- w_up: bfloat16 [960, 2560], P('fsdp', 'ctx'), may hold values from -0.1875 to 0.1875
- w_down: bfloat16 [2560, 960], P('fsdp', 'ctx'), may hold values from -0.125 to 0.125
- gain_attn: bfloat16 [960], P('ctx'), may hold values from 0.5 to 1.5
- gain_mlp: bfloat16 [960], P('ctx'), may hold values from 0.5 to 1.5
Outputs:
- output: bfloat16 [2, 2048, 960], P('fsdp', 'ctx')
- grad_input: bfloat16 [2, 2048, 960], P('fsdp', 'ctx')
- grad_w_query: float32 [960, 960], P('fsdp', 'ctx')
- grad_w_key: float32 [960, 320], P('fsdp', 'ctx')
- grad_w_value: float32 [960, 320], P('fsdp', 'ctx')
- grad_w_out: float32 [960, 960], P('fsdp', 'ctx')
- grad_w_gate: float32 [960, 2560], P('fsdp', 'ctx')
- grad_w_up: float32 [960, 2560], P('fsdp', 'ctx')
- grad_w_down: float32 [2560, 960], P('fsdp', 'ctx')
- grad_gain_attn: float32 [960], P('ctx')
- grad_gain_mlp: float32 [960], P('ctx')
All inputs are finite; a program needn't handle non-finite values.
Results may differ from a plain program's by a relative error of at most 0.018.
Values may be sent and summed in bfloat16 or wider, within the bound.
A program may use at most 256 MiB of HBM per device.

v0:
```python
import jax
import jax.numpy as jnp
from jax import lax
from jax.sharding import PartitionSpec as P

HEADS = 15
KV_HEADS = 5
HEAD = 64


EPSILON = 1e-05
ROPE_THETA = 100000.0


def tables(positions, head_size):
    half_size = head_size // 2
    frequency = ROPE_THETA ** (-jnp.arange(half_size, dtype=jnp.float32) * 2.0 / head_size)
    angles = positions.astype(jnp.float32)[:, None] * frequency[None, :]
    return (jnp.cos(angles), jnp.sin(angles))


def rotate(values, cosine, sine_table):
    half_size = values.shape[-1] // 2
    first_half = values[..., :half_size]
    second = values[..., half_size:]
    cosine = cosine[:, None, :]
    sine_table = sine_table[:, None, :]
    return jnp.concatenate(
        [first_half * cosine - second * sine_table, second * cosine + first_half * sine_table],
        axis=-1,
    )


def unrotate(values, cosine, sine_table):
    half_size = values.shape[-1] // 2
    first_half = values[..., :half_size]
    second = values[..., half_size:]
    cosine = cosine[:, None, :]
    sine_table = sine_table[:, None, :]
    return jnp.concatenate(
        [first_half * cosine + second * sine_table, second * cosine - first_half * sine_table],
        axis=-1,
    )


def normed(row_values, gain_vec):
    scale_rows = lax.rsqrt(jnp.mean(row_values * row_values, axis=-1, keepdims=True) + EPSILON)
    return row_values * scale_rows * gain_vec


def local(
    inputs, grad_output, w_query, w_key, w_value, w_out, w_gate, w_up, w_down, gain_attn, gain_mlp
):
    seq_count, block_len, model_width = inputs.shape
    row_count = seq_count * block_len
    cycle_size = lax.axis_size("ctx")
    cycle_index = lax.axis_index("ctx")
    length = block_len * cycle_size
    key_block = min(512, length)
    head_count = HEADS
    groups = KV_HEADS
    head_size = HEAD
    repeat_count = head_count // groups
    kv_width = groups * head_size
    positions = cycle_index * block_len + jnp.arange(block_len, dtype=jnp.int32)
    cosine, sine_table = tables(positions, head_size)
    cosine = jnp.tile(cosine, (seq_count, 1))
    sine_table = jnp.tile(sine_table, (seq_count, 1))
    needed = (cycle_index * block_len + block_len + key_block - 1) // key_block
    pieces_c = (
        lax.all_gather(w_query, "ctx", axis=1, tiled=True),
        lax.all_gather(w_key, "ctx", axis=1, tiled=True),
        lax.all_gather(w_value, "ctx", axis=1, tiled=True),
        lax.all_gather(w_out, "ctx", axis=1, tiled=True),
        lax.all_gather(w_gate, "ctx", axis=1, tiled=True),
        lax.all_gather(w_up, "ctx", axis=1, tiled=True),
        lax.all_gather(w_down, "ctx", axis=1, tiled=True),
        lax.all_gather(gain_attn, "ctx", axis=0, tiled=True),
        lax.all_gather(gain_mlp, "ctx", axis=0, tiled=True),
    )
    full_query, full_key, full_value, full_out, full_gate, full_up, full_down = (
        lax.all_gather(pieces_c[0], "fsdp", axis=0, tiled=True),
        lax.all_gather(pieces_c[1], "fsdp", axis=0, tiled=True),
        lax.all_gather(pieces_c[2], "fsdp", axis=0, tiled=True),
        lax.all_gather(pieces_c[3], "fsdp", axis=0, tiled=True),
        lax.all_gather(pieces_c[4], "fsdp", axis=0, tiled=True),
        lax.all_gather(pieces_c[5], "fsdp", axis=0, tiled=True),
        lax.all_gather(pieces_c[6], "fsdp", axis=0, tiled=True),
    )
    gain_first = pieces_c[7].astype(jnp.float32)
    gain_second = pieces_c[8].astype(jnp.float32)
    resid1 = inputs.reshape(row_count, model_width).astype(jnp.float32)
    normal1 = normed(resid1, gain_first).astype(jnp.bfloat16)
    query_raw = jnp.dot(normal1, full_query, preferred_element_type=jnp.float32).reshape(
        row_count, head_count, head_size
    )
    query_rot = rotate(query_raw, cosine, sine_table).astype(jnp.bfloat16)
    key_raw = jnp.dot(normal1, full_key, preferred_element_type=jnp.float32).reshape(
        row_count, groups, head_size
    )
    key_rows = (
        rotate(key_raw, cosine, sine_table)
        .astype(jnp.bfloat16)
        .reshape(seq_count, block_len, kv_width)
    )
    value_rows = (
        jnp.dot(normal1, full_value, preferred_element_type=jnp.float32)
        .astype(jnp.bfloat16)
        .reshape(seq_count, block_len, kv_width)
    )
    query_grouped = query_rot.reshape(seq_count, block_len, groups, repeat_count, head_size)
    peak_run = jnp.full((seq_count, groups, repeat_count, block_len), -1e30, jnp.float32)
    key_piece = lax.all_gather(key_rows, "ctx", axis=1, tiled=True)
    value_piece = lax.all_gather(value_rows, "ctx", axis=1, tiled=True)
    key_count = key_piece.shape[1]
    key_heads = key_piece.reshape(seq_count, key_count, groups, head_size)
    value_heads = value_piece.reshape(seq_count, key_count, groups, head_size)
    scores = (
        jnp.einsum(
            "sqgrd,skgd->sgrqk", query_grouped, key_heads, preferred_element_type=jnp.float32
        )
        * 0.125
    )
    allowed = jnp.arange(key_count, dtype=jnp.int32)[None, :] <= positions[:, None]
    scores = jnp.where(allowed, scores, -jnp.inf)
    new_peak = jnp.maximum(peak_run, jnp.max(scores, axis=-1))
    exp_terms = jnp.exp(scores - new_peak[..., None])
    denom_run = jnp.sum(exp_terms, axis=-1)
    running = jnp.einsum(
        "sgrqk,skgd->sgrqd",
        exp_terms.astype(jnp.bfloat16),
        value_heads,
        preferred_element_type=jnp.float32,
    )
    running, peak_run, denom_run = (running, new_peak, denom_run)
    attended = jnp.transpose(running / denom_run[..., None], (0, 3, 1, 2, 4)).astype(jnp.bfloat16)
    logsum = peak_run + jnp.log(denom_run)
    attended_rows = attended.reshape(row_count, head_count * head_size)
    resid2 = resid1 + jnp.dot(attended_rows, full_out, preferred_element_type=jnp.float32)
    normal2 = normed(resid2, gain_second).astype(jnp.bfloat16)
    gate_act = jnp.dot(normal2, full_gate, preferred_element_type=jnp.float32)
    up_act = jnp.dot(normal2, full_up, preferred_element_type=jnp.float32)
    hidden = (jax.nn.silu(gate_act) * up_act).astype(jnp.bfloat16)
    output = (resid2 + jnp.dot(hidden, full_down, preferred_element_type=jnp.float32)).astype(
        jnp.bfloat16
    )
    pieces_b = (
        lax.all_gather(w_query, "ctx", axis=1, tiled=True),
        lax.all_gather(w_key, "ctx", axis=1, tiled=True),
        lax.all_gather(w_value, "ctx", axis=1, tiled=True),
        lax.all_gather(w_out, "ctx", axis=1, tiled=True),
        lax.all_gather(w_gate, "ctx", axis=1, tiled=True),
        lax.all_gather(w_up, "ctx", axis=1, tiled=True),
        lax.all_gather(w_down, "ctx", axis=1, tiled=True),
        lax.all_gather(gain_attn, "ctx", axis=0, tiled=True),
        lax.all_gather(gain_mlp, "ctx", axis=0, tiled=True),
    )
    full_query, full_key, full_value, full_out, full_gate, full_up, full_down = (
        lax.all_gather(pieces_b[0], "fsdp", axis=0, tiled=True),
        lax.all_gather(pieces_b[1], "fsdp", axis=0, tiled=True),
        lax.all_gather(pieces_b[2], "fsdp", axis=0, tiled=True),
        lax.all_gather(pieces_b[3], "fsdp", axis=0, tiled=True),
        lax.all_gather(pieces_b[4], "fsdp", axis=0, tiled=True),
        lax.all_gather(pieces_b[5], "fsdp", axis=0, tiled=True),
        lax.all_gather(pieces_b[6], "fsdp", axis=0, tiled=True),
    )
    grad_rows = grad_output.reshape(row_count, model_width)
    grad_hidden = jnp.dot(grad_rows, full_down.T, preferred_element_type=jnp.float32)
    term_down = jnp.dot(hidden.T, grad_rows, preferred_element_type=jnp.float32)
    gate_sigma = jax.nn.sigmoid(gate_act)
    grad_up = (grad_hidden * gate_act * gate_sigma).astype(jnp.bfloat16)
    grad_gate = (grad_hidden * up_act * gate_sigma * (1.0 + gate_act * (1.0 - gate_sigma))).astype(
        jnp.bfloat16
    )
    term_gate = jnp.dot(normal2.T, grad_gate, preferred_element_type=jnp.float32)
    term_up = jnp.dot(normal2.T, grad_up, preferred_element_type=jnp.float32)
    grad_norm2 = jnp.dot(grad_gate, full_gate.T, preferred_element_type=jnp.float32) + jnp.dot(
        grad_up, full_up.T, preferred_element_type=jnp.float32
    )
    normed_out, pull_second = jax.vjp(normed, resid2, gain_second)
    grad_part2, term_gain2 = pull_second(grad_norm2)
    grad_resid2 = grad_rows.astype(jnp.float32) + grad_part2
    grad_branch = grad_resid2.astype(jnp.bfloat16)
    term_out = jnp.dot(attended_rows.T, grad_branch, preferred_element_type=jnp.float32)
    grad_attended = jnp.dot(grad_branch, full_out.T, preferred_element_type=jnp.float32).astype(
        jnp.bfloat16
    )
    grad_grouped = grad_attended.reshape(seq_count, block_len, groups, repeat_count, head_size)
    keys_all, values_all = (
        lax.all_gather(key_rows, "ctx", axis=1, tiled=True),
        lax.all_gather(value_rows, "ctx", axis=1, tiled=True),
    )

    def block_probs(key_start):
        key_heads = lax.dynamic_slice_in_dim(keys_all, key_start, key_block, 1).reshape(
            seq_count, key_block, groups, head_size
        )
        value_heads = lax.dynamic_slice_in_dim(values_all, key_start, key_block, 1).reshape(
            seq_count, key_block, groups, head_size
        )
        scores = (
            jnp.einsum(
                "sqgrd,skgd->sgrqk", query_grouped, key_heads, preferred_element_type=jnp.float32
            )
            * 0.125
        )
        allowed = (key_start + jnp.arange(key_block, dtype=jnp.int32))[None, :] <= positions[
            :, None
        ]
        scores = jnp.where(allowed, scores, -jnp.inf)
        prob_full = jnp.where(allowed, jnp.exp(scores - logsum[..., None]), 0.0)
        grad_probs = jnp.einsum(
            "sqgrd,skgd->sgrqk", grad_grouped, value_heads, preferred_element_type=jnp.float32
        )
        return (key_heads, prob_full, grad_probs)

    def delta_pass(step_index, delta_sum):
        key_heads, prob_full, grad_probs = block_probs(step_index * key_block)
        return delta_sum + jnp.sum(prob_full * grad_probs, axis=-1)

    row_delta = lax.fori_loop(
        0, needed, delta_pass, jnp.zeros((seq_count, groups, repeat_count, block_len), jnp.float32)
    )

    def retrace(step_index, loop_state):
        grad_query_acc, grad_keys_all, grad_values_all = loop_state
        key_start = step_index * key_block
        key_heads, prob_full, grad_probs = block_probs(key_start)
        grad_scores = (prob_full * (grad_probs - row_delta[..., None]) * 0.125).astype(jnp.bfloat16)
        prob_low = prob_full.astype(jnp.bfloat16)
        value_term = jnp.einsum(
            "sgrqk,sqgrd->skgd", prob_low, grad_grouped, preferred_element_type=jnp.float32
        ).reshape(seq_count, key_block, kv_width)
        key_term = jnp.einsum(
            "sgrqk,sqgrd->skgd", grad_scores, query_grouped, preferred_element_type=jnp.float32
        ).reshape(seq_count, key_block, kv_width)
        grad_query_acc = grad_query_acc + jnp.einsum(
            "sgrqk,skgd->sgrqd", grad_scores, key_heads, preferred_element_type=jnp.float32
        )
        grad_keys_all = lax.dynamic_update_slice_in_dim(grad_keys_all, key_term, key_start, 1)
        grad_values_all = lax.dynamic_update_slice_in_dim(grad_values_all, value_term, key_start, 1)
        return (grad_query_acc, grad_keys_all, grad_values_all)

    back_state = (
        jnp.zeros((seq_count, groups, repeat_count, block_len, head_size), jnp.float32),
        jnp.zeros((seq_count, length, kv_width), jnp.float32),
        jnp.zeros((seq_count, length, kv_width), jnp.float32),
    )
    grad_query_acc, grad_keys_all, grad_values_all = lax.fori_loop(0, needed, retrace, back_state)
    grad_keys_own, grad_values_own = (
        lax.psum_scatter(grad_keys_all, "ctx", scatter_dimension=1, tiled=True),
        lax.psum_scatter(grad_values_all, "ctx", scatter_dimension=1, tiled=True),
    )
    grad_query_rows = jnp.transpose(grad_query_acc, (0, 3, 1, 2, 4)).reshape(
        row_count, head_count, head_size
    )
    grad_query = (
        unrotate(grad_query_rows, cosine, sine_table)
        .reshape(row_count, head_count * head_size)
        .astype(jnp.bfloat16)
    )
    grad_keys = (
        unrotate(grad_keys_own.reshape(row_count, groups, head_size), cosine, sine_table)
        .reshape(row_count, kv_width)
        .astype(jnp.bfloat16)
    )
    grad_values = grad_values_own.reshape(row_count, kv_width).astype(jnp.bfloat16)
    term_query = jnp.dot(normal1.T, grad_query, preferred_element_type=jnp.float32)
    term_key = jnp.dot(normal1.T, grad_keys, preferred_element_type=jnp.float32)
    term_value = jnp.dot(normal1.T, grad_values, preferred_element_type=jnp.float32)
    grad_norm1 = jnp.dot(grad_query, full_query.T, preferred_element_type=jnp.float32)
    grad_norm1 = grad_norm1 + jnp.dot(grad_keys, full_key.T, preferred_element_type=jnp.float32)
    grad_norm1 = grad_norm1 + jnp.dot(grad_values, full_value.T, preferred_element_type=jnp.float32)
    normed_first, pull_first = jax.vjp(normed, resid1, gain_first)
    grad_part1, term_gain1 = pull_first(grad_norm1)
    grad_input = (
        (grad_resid2 + grad_part1).astype(jnp.bfloat16).reshape(seq_count, block_len, model_width)
    )
    gain_sum1, gain_sum2 = lax.psum((term_gain1, term_gain2), "fsdp")
    halves = (
        lax.psum_scatter(
            term_query.astype(jnp.bfloat16), "fsdp", scatter_dimension=0, tiled=True
        ).astype(jnp.float32),
        lax.psum_scatter(
            term_key.astype(jnp.bfloat16), "fsdp", scatter_dimension=0, tiled=True
        ).astype(jnp.float32),
        lax.psum_scatter(
            term_value.astype(jnp.bfloat16), "fsdp", scatter_dimension=0, tiled=True
        ).astype(jnp.float32),
        lax.psum_scatter(
            term_out.astype(jnp.bfloat16), "fsdp", scatter_dimension=0, tiled=True
        ).astype(jnp.float32),
        lax.psum_scatter(
            term_gate.astype(jnp.bfloat16), "fsdp", scatter_dimension=0, tiled=True
        ).astype(jnp.float32),
        lax.psum_scatter(
            term_up.astype(jnp.bfloat16), "fsdp", scatter_dimension=0, tiled=True
        ).astype(jnp.float32),
        lax.psum_scatter(
            term_down.astype(jnp.bfloat16), "fsdp", scatter_dimension=0, tiled=True
        ).astype(jnp.float32),
    )
    sums = (
        lax.psum_scatter(halves[0], "ctx", scatter_dimension=1, tiled=True),
        lax.psum_scatter(halves[1], "ctx", scatter_dimension=1, tiled=True),
        lax.psum_scatter(halves[2], "ctx", scatter_dimension=1, tiled=True),
        lax.psum_scatter(halves[3], "ctx", scatter_dimension=1, tiled=True),
        lax.psum_scatter(halves[4], "ctx", scatter_dimension=1, tiled=True),
        lax.psum_scatter(halves[5], "ctx", scatter_dimension=1, tiled=True),
        lax.psum_scatter(halves[6], "ctx", scatter_dimension=1, tiled=True),
        lax.psum_scatter(gain_sum1, "ctx", scatter_dimension=0, tiled=True),
        lax.psum_scatter(gain_sum2, "ctx", scatter_dimension=0, tiled=True),
    )
    return (
        output.reshape(seq_count, block_len, model_width),
        grad_input,
        sums[0],
        sums[1],
        sums[2],
        sums[3],
        sums[4],
        sums[5],
        sums[6],
        sums[7],
        sums[8],
    )


def solution(mesh):
    return jax.shard_map(
        local,
        mesh=mesh,
        in_specs=(
            P("fsdp", "ctx", None),
            P("fsdp", "ctx", None),
            P("fsdp", "ctx"),
            P("fsdp", "ctx"),
            P("fsdp", "ctx"),
            P("fsdp", "ctx"),
            P("fsdp", "ctx"),
            P("fsdp", "ctx"),
            P("fsdp", "ctx"),
            P("ctx"),
            P("ctx"),
        ),
        out_specs=(
            P("fsdp", "ctx", None),
            P("fsdp", "ctx", None),
            P("fsdp", "ctx"),
            P("fsdp", "ctx"),
            P("fsdp", "ctx"),
            P("fsdp", "ctx"),
            P("fsdp", "ctx"),
            P("fsdp", "ctx"),
            P("fsdp", "ctx"),
            P("ctx"),
            P("ctx"),
        ),
        check_vma=False,
    )
```

profile of v0, /device:TPU:0, one launch (start us, length us, event | category | flops | bytes accessed | tf_op | source)
XLA Modules:
  0.0 1180.1 jit_solution(13564911605797883869)
XLA Ops:
  8.7 26.8 %all-gather.3 = bf16[16,60,480]{2,1,0:T(8,128)(2,1)S(1)} all-gather(bf16[1,60,480]{2,1,0:T(8,128)(2,1)} %bitcast.423), channel_id=1, replica_groups=mesh['fsdp'=2,'ctx'=16] {'ctx'}, dimensions={0}, use_global_device_ids=true | all-gather | bytes 979200 | tf_op jit(solution)/shard_map/all_gather | solution.py:71
  39.9 30.6 %all-reduce.14 = (bf16[960]{0:T(1024)(128)(2,1)S(1)}, bf16[960]{0:T(1024)(128)(2,1)S(1)}) all-reduce(bf16[960]{0:T(1024)(128)(2,1)S(1)} %dynamic-update-slice, bf16[960]{0:T(1024)(128)(2,1)S(1)} %dynamic-update-slice.1), channel_id=1, replica_groups=mesh['fsdp'=2,'ctx'=16] {'ctx'}, use_global_device_ids=true, to_apply=%add | all-reduce | flops 1920 | bytes 7680
  70.5 18.9 %all-gather.1 = bf16[16,20,480]{2,1,0:T(8,128)(2,1)S(1)} all-gather(bf16[1,20,480]{2,1,0:T(8,128)(2,1)S(1)} %bitcast.425), channel_id=1, replica_groups=mesh['fsdp'=2,'ctx'=16] {'ctx'}, dimensions={0}, use_global_device_ids=true | all-gather | bytes 326400 | tf_op jit(solution)/shard_map/all_gather | solution.py:72
  89.5 10.6 all-gather.2
  103.1 20.1 %all-gather.4 = bf16[16,20,480]{2,1,0:T(8,128)(2,1)S(1)} all-gather(bf16[1,20,480]{2,1,0:T(8,128)(2,1)S(1)} %bitcast.426), channel_id=1, replica_groups=mesh['fsdp'=2,'ctx'=16] {'ctx'}, dimensions={0}, use_global_device_ids=true | all-gather | bytes 326400 | tf_op jit(solution)/shard_map/all_gather | solution.py:73
  123.3 17.7 %all-gather.5 = bf16[2,480,320]{1,2,0:T(8,128)(2,1)S(1)} all-gather(bf16[1,480,320]{1,2,0:T(8,128)(2,1)S(1)} %bitcast.409), channel_id=1, replica_groups=mesh['fsdp'=2,'ctx'=16] {'fsdp'}, dimensions={0}, use_global_device_ids=true | all-gather | bytes 921600 | tf_op jit(solution)/shard_map/all_gather | solution.py:84
  143.6 22.5 %all-gather.6 = bf16[16,60,480]{2,1,0:T(8,128)(2,1)S(1)} all-gather(bf16[1,60,480]{2,1,0:T(8,128)(2,1)S(1)} %bitcast.424), channel_id=1, replica_groups=mesh['fsdp'=2,'ctx'=16] {'ctx'}, dimensions={0}, use_global_device_ids=true | all-gather | bytes 979200 | tf_op jit(solution)/shard_map/all_gather | solution.py:74
  181.3 7.1 all-gather.37.cloned.1.call-done
  192.8 34.6 %all-gather.19.cloned.1.call-done = bf16[1,2048,320]{1,2,0:T(8,128)(2,1)} async-done(((bf16[1,128,320]{1,2,0:T(8,128)(2,1)}), bf16[1,2048,320]{1,2,0:T(8,128)(2,1)}) %all-gather.19.cloned.1.call-update) | async-done | bytes 1310736 | tf_op jit(solution)/shard_map/all_gather | solution.py:113
  227.4 9.1 fusion.45
  236.5 8.7 fusion.43
  245.2 21.7 %all-gather.35.cloned.1.call-done = bf16[2048,320]{0,1:T(8,128)(2,1)} async-done(((bf16[128,320]{0,1:T(8,128)(2,1)}), bf16[2048,320]{0,1:T(8,128)(2,1)}) %all-gather.35.cloned.1.call-update) | async-done | bytes 1310736 | tf_op jit(solution)/shard_map/all_gather | solution.py:114
  266.8 9.6 fusion.56
  276.4 22.9 %all-gather.23.cloned.1.call-done = bf16[960,960]{1,0:T(8,128)(2,1)} async-done(((bf16[480,960]{1,0:T(8,128)(2,1)}), bf16[960,960]{1,0:T(8,128)(2,1)}) %all-gather.23.cloned.1.call-update) | async-done | bytes 1843216 | tf_op jit(solution)/shard_map/all_gather | solution.py:85
  302.6 63.2 %all-gather.27.cloned.1.call-done = bf16[960,2560]{1,0:T(8,128)(2,1)} async-done(((bf16[480,2560]{1,0:T(8,128)(2,1)}), bf16[960,2560]{1,0:T(8,128)(2,1)}) %all-gather.27.cloned.1.call-update) | async-done | bytes 4915216 | tf_op jit(solution)/shard_map/all_gather | solution.py:86
  370.1 62.1 %all-gather.31.cloned.1.call-done = bf16[960,2560]{1,0:T(8,128)(2,1)} async-done(((bf16[480,2560]{1,0:T(8,128)(2,1)}), bf16[960,2560]{1,0:T(8,128)(2,1)}) %all-gather.31.cloned.1.call-update) | async-done | bytes 4915216 | tf_op jit(solution)/shard_map/all_gather | solution.py:87
  436.5 61.9 %all-gather.33.cloned.1.call-done = bf16[2560,960]{0,1:T(8,128)(2,1)} async-done(((bf16[1280,960]{0,1:T(8,128)(2,1)}), bf16[2560,960]{0,1:T(8,128)(2,1)}) %all-gather.33.cloned.1.call-update) | async-done | bytes 4915216 | tf_op jit(solution)/shard_map/all_gather | solution.py:88
  498.4 5.8 multiply_convert_fusion
  521.0 7.1 while.27
  542.5 81.6 %reduce-scatter.28.cloned.1.call-done = f32[1,128,320]{1,2,0:T(8,128)} async-done(((f32[1,2048,320]{1,2,0:T(8,128)}), f32[1,128,320]{1,2,0:T(8,128)}) %reduce-scatter.28.cloned.1.call-update) | async-done | bytes 163856 | tf_op jit(solution)/shard_map/reduce_scatter | solution.py:251
  626.8 64.1 %reduce-scatter.30.cloned.1.call-done = f32[1,128,320]{1,2,0:T(8,128)} async-done(((f32[1,2048,320]{1,2,0:T(8,128)}), f32[1,128,320]{1,2,0:T(8,128)}) %reduce-scatter.30.cloned.1.call-update) | async-done | bytes 163856 | tf_op jit(solution)/shard_map/reduce_scatter | solution.py:252
  697.3 57.2 %reduce-scatter.36.cloned.1.call-done = bf16[480,2560]{1,0:T(8,128)(2,1)} async-done(((bf16[960,2560]{1,0:T(8,128)(2,1)}), bf16[480,2560]{1,0:T(8,128)(2,1)}) %reduce-scatter.36.cloned.1.call-update) | async-done | bytes 2457616 | tf_op jit(solution)/shard_map/reduce_scatter | solution.py:293
  754.5 4.9 copy.100
  759.5 59.5 %reduce-scatter.38.cloned.1.call-done = bf16[480,2560]{1,0:T(8,128)(2,1)} async-done(((bf16[960,2560]{1,0:T(8,128)(2,1)}), bf16[480,2560]{1,0:T(8,128)(2,1)}) %reduce-scatter.38.cloned.1.call-update) | async-done | bytes 2457616 | tf_op jit(solution)/shard_map/reduce_scatter | solution.py:296
  825.2 5.5 fusion.52
  830.7 20.9 %reduce-scatter.32.cloned.1.call-done = bf16[480,960]{1,0:T(8,128)(2,1)} async-done(((bf16[960,960]{1,0:T(8,128)(2,1)}), bf16[480,960]{1,0:T(8,128)(2,1)}) %reduce-scatter.32.cloned.1.call-update) | async-done | bytes 921616 | tf_op jit(solution)/shard_map/reduce_scatter | solution.py:281
  851.6 32.6 %reduce-scatter.34.cloned.1.call-done = bf16[480,960]{1,0:T(8,128)(2,1)} async-done(((bf16[960,960]{1,0:T(8,128)(2,1)}), bf16[480,960]{1,0:T(8,128)(2,1)}) %reduce-scatter.34.cloned.1.call-update) | async-done | bytes 921616 | tf_op jit(solution)/shard_map/reduce_scatter | solution.py:290
  888.1 92.9 %all-reduce.17 = (f32[480,960]{1,0:T(8,128)}, f32[480,960]{1,0:T(8,128)}, f32[960]{0:T(1024)S(1)}, f32[960]{0:T(1024)S(1)}) all-reduce(bf16[480,960]{1,0:T(8,128)(2,1)} %reduce-scatter.32.cloned.1.call-done, bf16[480,960]{1,0:T(8,128)(2,1)} %reduce-scatter.34.cloned.1.call-done, ...), channel_id=6, replica_groups=mesh['fsdp'=2,'ctx'=16] {'ctx'}, use_global_device_ids=true, to_apply=%region_14.15.clone | all-reduce | flops 923520 | bytes 5544960
  991.2 86.8 %fusion.110 = (f32[480,24]{0,1:T(8,128)S(1)}, f32[480,24]{0,1:T(8,128)S(1)}, f32[1280,64]{0,1:T(8,128)S(1)}) fusion(f32[480,320]{0,1:T(8,128)S(1)} %convert_element_type.214, f32[480,320]{0,1:T(8,128)S(1)} %convert_element_type.216, f32[1280,960]{0,1:T(8,128)} %convert_element_type.224), kind=kCustom, calls=%all-reduce-scatter.3 | all-reduce-scatter fusion | flops 1679362 | bytes 6564352
  1078.0 12.9 %collective-permute-start.1 = (f32[480,24]{0,1:T(8,128)S(1)}, f32[480,24]{0,1:T(8,128)S(1)}, u32[]{:S(2)}, u32[]{:S(2)}) collective-permute-start(f32[480,24]{0,1:T(8,128)S(1)} %get-tuple-element.290), channel_id=1, source_target_pairs={{0,2},{1,3},{2,4},{3,5},{4,6},{5,7},{6,8},{7,9},{8,10},{9,11},{10,... | collective-permute-start | bytes 138248
  1109.3 5.4 all-reduce.13
  1118.0 55.1 %reduce-scatter.48.cloned.1.call-done = f32[160,480]{1,0:T(8,128)} async-done(((f32[2560,480]{1,0:T(8,128)}), f32[160,480]{1,0:T(8,128)}) %reduce-scatter.48.cloned.1.call-update) | async-done | bytes 307216
  (250 shorter events, 132.7 us)
Async XLA Ops:
  7.2 160.8 %all-gather.25.cloned.1.call-start = ((), (), s32[]{:S(2)}) async-start(), calls=%async_computation.14 | async-start | bytes 2785280 | tf_op jit(solution)/shard_map/all_gather | solution.py:75
  8.0 164.8 %all-gather.29.cloned.1.call-start = ((), (), s32[]{:S(2)}) async-start(), calls=%async_computation.16 | async-start | bytes 2785280 | tf_op jit(solution)/shard_map/all_gather | solution.py:76
  8.7 168.8 %all-gather.21.cloned.1.call-start = ((), (), s32[]{:S(2)}) async-start(), calls=%async_computation.12 | async-start | bytes 2949120 | tf_op jit(solution)/shard_map/all_gather | solution.py:82
  37.5 151.0 %all-gather.37.cloned.1.call-start = ((), (), s32[]{:S(2)}) async-start(), calls=%async_computation.27 | async-start | bytes 2785280 | tf_op jit(solution)/shard_map/all_gather | solution.py:77
  38.1 189.3 %all-gather.19.cloned.1.call-start = ((), (), s32[]{:S(2)}) async-start(), calls=%async_computation.11 | async-start | bytes 1392640 | tf_op jit(solution)/shard_map/all_gather | solution.py:113
  103.0 163.8 %all-gather.35.cloned.1.call-start = ((), (), s32[]{:S(2)}) async-start(), calls=%async_computation.26 | async-start | bytes 1392640 | tf_op jit(solution)/shard_map/all_gather | solution.py:114
  143.5 155.8 %all-gather.23.cloned.1.call-start = ((), (), s32[]{:S(2)}) async-start(), calls=%async_computation.13 | async-start | bytes 2949120 | tf_op jit(solution)/shard_map/all_gather | solution.py:85
  168.0 197.8 %all-gather.27.cloned.1.call-start = ((), (), s32[]{:S(2)}) async-start(), calls=%async_computation.15 | async-start | bytes 7372800 | tf_op jit(solution)/shard_map/all_gather | solution.py:86
  172.6 259.5 %all-gather.31.cloned.1.call-start = ((), (), s32[]{:S(2)}) async-start(), calls=%async_computation.17 | async-start | bytes 7372800 | tf_op jit(solution)/shard_map/all_gather | solution.py:87
  177.3 321.2 %all-gather.33.cloned.1.call-start = ((), (), s32[]{:S(2)}) async-start(), calls=%async_computation.18 | async-start | bytes 7372800 | tf_op jit(solution)/shard_map/all_gather | solution.py:88
  177.3 331.3 %copy-start.24 = (f32[960]{0:T(1024)}, f32[960]{0:T(1024)S(1)}, u32[]{:S(2)}) copy-start(f32[960]{0:T(1024)S(1)} %convert_element_type.195) | copy-start | bytes 11524
  192.6 431.6 %reduce-scatter.28.cloned.1.call-start = ((), (), s32[]{:S(2)}) async-start(), calls=%async_computation.19 | async-start | bytes 2785280 | tf_op jit(solution)/shard_map/reduce_scatter | solution.py:251
  301.8 206.8 %copy-start.34 = (f32[128]{0:T(128)}, f32[128]{0:T(128)S(1)}, u32[]{:S(2)}) copy-start(f32[128]{0:T(128)S(1)} %fusion.100) | copy-start | bytes 1540
  528.1 162.9 %reduce-scatter.30.cloned.1.call-start = ((), (), s32[]{:S(2)}) async-start(), calls=%async_computation.20 | async-start | bytes 2785280 | tf_op jit(solution)/shard_map/reduce_scatter | solution.py:252
  528.7 225.8 %reduce-scatter.36.cloned.1.call-start = ((), (), s32[]{:S(2)}) async-start(), calls=%async_computation.23 | async-start | bytes 7372800 | tf_op jit(solution)/shard_map/reduce_scatter | solution.py:293
  532.9 286.1 %reduce-scatter.38.cloned.1.call-start = ((), (), s32[]{:S(2)}) async-start(), calls=%async_computation.24 | async-start | bytes 7372800 | tf_op jit(solution)/shard_map/reduce_scatter | solution.py:296
  537.7 313.9 %reduce-scatter.32.cloned.1.call-start = ((), (), s32[]{:S(2)}) async-start(), calls=%async_computation.21 | async-start | bytes 2949120 | tf_op jit(solution)/shard_map/reduce_scatter | solution.py:281
  540.4 343.7 %reduce-scatter.34.cloned.1.call-start = ((), (), s32[]{:S(2)}) async-start(), calls=%async_computation.22 | async-start | bytes 2949120 | tf_op jit(solution)/shard_map/reduce_scatter | solution.py:290
  542.4 151.2 %copy-start.6 = (bf16[128,2560]{1,0:T(8,128)(2,1)S(1)}, bf16[128,2560]{1,0:T(8,128)(2,1)}, u32[]{:S(2)}) copy-start(bf16[128,2560]{1,0:T(8,128)(2,1)} %get-tuple-element.299) | copy-start | bytes 1966084
  542.4 151.2 %copy-start.14 = (bf16[1,128,960]{1,2,0:T(8,128)(2,1)S(1)}, bf16[1,128,960]{1,2,0:T(8,128)(2,1)}, u32[]{:S(2)}) copy-start(bf16[1,128,960]{1,2,0:T(8,128)(2,1)} %param.16) | copy-start | bytes 737284
  542.5 438.6 %reduce-scatter.42.cloned.1.call-start = ((), (), s32[]{:S(2)}) async-start(), calls=%async_computation.28 | async-start | bytes 1105920
  626.8 355.5 %reduce-scatter.44.cloned.1.call-start = ((), (), s32[]{:S(2)}) async-start(), calls=%async_computation.29 | async-start | bytes 1105920
  693.5 293.4 %reduce-scatter.40.cloned.1.call-start = ((), (), s32[]{:S(2)}) async-start(), calls=%async_computation.25 | async-start | bytes 7372800 | tf_op jit(solution)/shard_map/reduce_scatter | solution.py:299
  697.3 420.7 %reduce-scatter.46.cloned.1.call-start = ((), (), s32[]{:S(2)}) async-start(), calls=%async_computation.30 | async-start | bytes 5570560
  759.5 413.6 %reduce-scatter.48.cloned.1.call-start = ((), (), s32[]{:S(2)}) async-start(), calls=%async_computation.31 | async-start | bytes 5570560
  1078.0 25.8 %collective-permute-start.1 = (f32[480,24]{0,1:T(8,128)S(1)}, f32[480,24]{0,1:T(8,128)S(1)}, u32[]{:S(2)}, u32[]{:S(2)}) collective-permute-start(f32[480,24]{0,1:T(8,128)S(1)} %get-tuple-element.290), channel_id=1, source_target_pairs={{0,2},{1,3},{2,4},{3,5},{4,6},{5,7},{6,8},{7,9},{8,10},{9,11},{10,... | collective-permute-start | bytes 138248
  1090.9 9.7 collective-permute-start.2
  1093.1 21.5 %collective-permute-start = (f32[480,24]{0,1:T(8,128)S(1)}, f32[480,24]{0,1:T(8,128)S(1)}, u32[]{:S(2)}, u32[]{:S(2)}) collective-permute-start(f32[480,24]{0,1:T(8,128)S(1)} %get-tuple-element.290), channel_id=1, source_target_pairs={{0,1},{1,2},{2,3},{3,4},{4,5},{5,6},{6,7},{7,8},{8,9},{9,10},{10,1... | collective-permute-start | bytes 138248
  1095.5 19.6 %collective-permute-start.4 = (f32[480,24]{0,1:T(8,128)S(1)}, f32[480,24]{0,1:T(8,128)S(1)}, u32[]{:S(2)}, u32[]{:S(2)}) collective-permute-start(f32[480,24]{0,1:T(8,128)S(1)} %get-tuple-element.291), channel_id=1, source_target_pairs={{0,2},{1,3},{2,4},{3,5},{4,6},{5,7},{6,8},{7,9},{8,10},{9,11},{10,... | collective-permute-start | bytes 138248
  1097.5 17.6 %collective-permute-start.3 = (f32[480,24]{0,1:T(8,128)S(1)}, f32[480,24]{0,1:T(8,128)S(1)}, u32[]{:S(2)}, u32[]{:S(2)}) collective-permute-start(f32[480,24]{0,1:T(8,128)S(1)} %get-tuple-element.291), channel_id=1, source_target_pairs={{0,1},{1,2},{2,3},{3,4},{4,5},{5,6},{6,7},{7,8},{8,9},{9,10},{10,1... | collective-permute-start | bytes 138248
  1100.6 14.5 %collective-permute-start.5 = (f32[480,12]{0,1:T(8,128)S(1)}, f32[480,12]{0,1:T(8,128)S(1)}, u32[]{:S(2)}, u32[]{:S(2)}) collective-permute-start(f32[480,12]{0,1:T(8,128)S(1)} %slice.41), channel_id=1, source_target_pairs={{0,3},{1,4},{2,5},{3,6},{4,7},{5,8},{6,9},{7,10},{8,11},{9,12},{10... | collective-permute-start | bytes 69128
  1103.8 13.0 %collective-permute-start.6 = (f32[1280,60]{0,1:T(8,128)S(1)}, f32[1280,60]{0,1:T(8,128)S(1)}, u32[]{:S(2)}, u32[]{:S(2)}) collective-permute-start(f32[1280,60]{0,1:T(8,128)S(1)} %slice.42), channel_id=1, source_target_pairs={{0,1},{1,2},{2,3},{3,4},{4,5},{5,6},{6,7},{7,8},{8,9},{9,10},{10,1... | collective-permute-start | bytes 921608
  (36 other events, 1148.7 us)
Sparse Core Ops, SparseCore 0:
  10.3 47.6 all-gather.24
  60.2 41.9 all-gather.28
  103.8 37.4 all-gather.20
  143.4 44.9 all-gather.36
  191.0 36.3 all-gather.18
  230.0 36.8 all-gather.34
  268.4 30.8 all-gather.22
  300.9 64.8 all-gather.26
  367.3 64.8 all-gather.30
  433.6 64.8 all-gather.32
  528.2 95.8 reduce-scatter.27
  627.8 63.1 reduce-scatter.29
  693.3 61.2 reduce-scatter.35
  756.7 62.1 reduce-scatter.37
  821.0 30.4 reduce-scatter.31
  853.6 30.4 reduce-scatter.33
  886.2 16.9 reduce-scatter.41
  905.4 16.9 reduce-scatter.43
  924.7 62.1 reduce-scatter.39
  991.2 100.2 reduce-scatter.45
  1095.9 77.0 reduce-scatter.47
where the time goes:
time: 1190 us; the launch traced here: 1180 us
  waiting for transfers between devices  651 us (55%)
  blocking collectives  332 us (28%)
  matrix products  78.7 us (7%)
  local copies, waits for them, and re-layouts  54.1 us (5%)
  starting transfers between devices  28.3 us (2%)
  other arithmetic  18.4 us (2%)
  between operations  17.4 us (1%)
    unnamed x3, blocking collectives  210 us
    reduce_scatter x1, waiting for transfers between devices, local(): lax.psum_scatter(grad_keys_all, 'ctx', scatter_dimension=1, tiled=True)  81.6 us
    reduce_scatter x1, waiting for transfers between devices, local(): lax.psum_scatter(grad_values_all, 'ctx', scatter_dimension=1, tiled=True)  64.1 us
    all_gather x1, waiting for transfers between devices, local(): lax.all_gather(pieces_c[4], 'fsdp', axis=0, tiled=True)  63.2 us
    all_gather x1, waiting for transfers between devices, local(): lax.all_gather(pieces_c[5], 'fsdp', axis=0, tiled=True)  62.1 us
    all_gather x1, waiting for transfers between devices, local(): lax.all_gather(pieces_c[6], 'fsdp', axis=0, tiled=True)  61.9 us
    reduce_scatter x1, waiting for transfers between devices, local(): lax.psum_scatter(term_up.astype(jnp.bfloat16), 'fsdp', scatter_dimension=...  59.5 us
    unnamed x32, waiting for transfers between devices  57.8 us
  transfers between devices with their start and end apart: 28, of which 15 were waited for; matrix products, arithmetic and copies ran while one was open for 18% of the time, Pallas kernels for 0%

commit v1 on v0

v1 whole, which is shorter than its diff:
```python
import jax
import jax.numpy as jnp
from jax import lax
from jax.sharding import PartitionSpec as P

HEADS = 15
KV_HEADS = 5
HEAD = 64


EPSILON = 1e-05
ROPE_THETA = 100000.0


def tables(positions, head_size):
    half_size = head_size // 2
    frequency = ROPE_THETA ** (-jnp.arange(half_size, dtype=jnp.float32) * 2.0 / head_size)
    angles = positions.astype(jnp.float32)[:, None] * frequency[None, :]
    return (jnp.cos(angles), jnp.sin(angles))


def rotate(values, cosine, sine_table):
    half_size = values.shape[-1] // 2
    first_half = values[..., :half_size]
    second = values[..., half_size:]
    cosine = cosine[:, None, :]
    sine_table = sine_table[:, None, :]
    return jnp.concatenate(
        [first_half * cosine - second * sine_table, second * cosine + first_half * sine_table],
        axis=-1,
    )


def unrotate(values, cosine, sine_table):
    half_size = values.shape[-1] // 2
    first_half = values[..., :half_size]
    second = values[..., half_size:]
    cosine = cosine[:, None, :]
    sine_table = sine_table[:, None, :]
    return jnp.concatenate(
        [first_half * cosine + second * sine_table, second * cosine - first_half * sine_table],
        axis=-1,
    )


def normed(row_values, gain_vec):
    scale_rows = lax.rsqrt(jnp.mean(row_values * row_values, axis=-1, keepdims=True) + EPSILON)
    return row_values * scale_rows * gain_vec


BOTH = ("fsdp", "ctx")


def forward_dot(pieces, halves):
    total = None
    for piece, half in zip(pieces, halves):
        term = lax.dot_general(
            piece, half, (((1,), (1,)), ((), ())), preferred_element_type=jnp.float32
        )
        total = term if total is None else total + term
    return total


def backward_dot(grads, halves):
    return jnp.concatenate(
        [jnp.dot(grads, half, preferred_element_type=jnp.float32) for half in halves], axis=-1
    )


def weight_terms(grads, pieces, cycle_size):
    terms = [
        lax.dot_general(
            grads, piece, (((0,), (0,)), ((), ())), preferred_element_type=jnp.float32
        ).astype(jnp.bfloat16)
        for piece in pieces
    ]
    return jnp.stack(
        [term.reshape(cycle_size, term.shape[0] // cycle_size, term.shape[1]) for term in terms]
    )


def cut(rows, count):
    return jnp.split(rows, count, axis=-1)


def gather_rows(packed, split_count, cycle_size):
    gathered = lax.all_gather(packed, BOTH, axis=0, tiled=False)
    return gathered.reshape(split_count, cycle_size, *packed.shape)


def take(gathered, start, size):
    piece = lax.slice_in_dim(gathered, start, start + size, axis=2)
    return [part.reshape(-1, part.shape[-1]) for part in piece]


def scatter_rows(terms):
    merged = terms.reshape(-1, *terms.shape[2:])
    return lax.psum_scatter(merged, BOTH, scatter_dimension=0, tiled=True)[0].astype(jnp.float32)


def local(
    inputs, grad_output, w_query, w_key, w_value, w_out, w_gate, w_up, w_down, gain_attn, gain_mlp
):
    seq_count, block_len, model_width = inputs.shape
    row_count = seq_count * block_len
    split_count = lax.axis_size("fsdp")
    cycle_size = lax.axis_size("ctx")
    cycle_index = lax.axis_index("ctx")
    length = block_len * cycle_size
    key_block = min(512, length)
    groups = KV_HEADS
    head_size = HEAD
    repeat_count = HEADS // KV_HEADS
    kv_width = groups * head_size
    positions = cycle_index * block_len + jnp.arange(block_len, dtype=jnp.int32)
    cosine, sine_table = tables(positions, head_size)
    cosine = jnp.tile(cosine, (seq_count, 1))
    sine_table = jnp.tile(sine_table, (seq_count, 1))
    needed = (cycle_index * block_len + block_len + key_block - 1) // key_block
    wide_q, wide_k, wide_v = w_query.shape[1], w_key.shape[1], w_value.shape[1]
    wide_o, wide_g, wide_u = w_out.shape[1], w_gate.shape[1], w_up.shape[1]
    part_width = w_query.shape[0]
    gain_size = gain_attn.shape[0]
    gain_row = jnp.pad(
        jnp.concatenate([gain_attn, gain_mlp]), (0, part_width - 2 * gain_size)
    )[None, :]
    packed_first = jnp.concatenate([w_query.T, w_key.T, w_value.T, gain_row], axis=0)
    packed_rest = jnp.concatenate([w_out.T, w_gate.T, w_up.T], axis=0)
    first = gather_rows(packed_first, split_count, cycle_size)
    rest = gather_rows(packed_rest, split_count, cycle_size)
    down = gather_rows(w_down.T, split_count, cycle_size)
    full_query = take(first, 0, wide_q)
    full_key = take(first, wide_q, wide_k)
    full_value = take(first, wide_q + wide_k, wide_v)
    gain_rows = first[0, :, wide_q + wide_k + wide_v, :]
    gain_first = gain_rows[:, :gain_size].reshape(-1).astype(jnp.float32)
    gain_second = gain_rows[:, gain_size : 2 * gain_size].reshape(-1).astype(jnp.float32)
    full_out = take(rest, 0, wide_o)
    full_gate = take(rest, wide_o, wide_g)
    full_up = take(rest, wide_o + wide_g, wide_u)
    full_down = take(down, 0, w_down.shape[1])

    resid1 = inputs.reshape(row_count, model_width).astype(jnp.float32)
    normal1 = normed(resid1, gain_first).astype(jnp.bfloat16)
    normal1_parts = cut(normal1, split_count)
    query_raw = forward_dot(normal1_parts, full_query).reshape(row_count, HEADS, head_size)
    query_rot = rotate(query_raw, cosine, sine_table).astype(jnp.bfloat16)
    key_raw = forward_dot(normal1_parts, full_key).reshape(row_count, groups, head_size)
    key_rows = (
        rotate(key_raw, cosine, sine_table)
        .astype(jnp.bfloat16)
        .reshape(seq_count, block_len, kv_width)
    )
    value_rows = (
        forward_dot(normal1_parts, full_value)
        .astype(jnp.bfloat16)
        .reshape(seq_count, block_len, kv_width)
    )
    query_grouped = query_rot.reshape(seq_count, block_len, groups, repeat_count, head_size)
    pair_all = lax.all_gather(
        jnp.concatenate([key_rows, value_rows], axis=-1), "ctx", axis=1, tiled=True
    )
    keys_all = pair_all[..., :kv_width]
    values_all = pair_all[..., kv_width:]
    key_heads = keys_all.reshape(seq_count, length, groups, head_size)
    value_heads = values_all.reshape(seq_count, length, groups, head_size)
    scores = (
        jnp.einsum(
            "sqgrd,skgd->sgrqk", query_grouped, key_heads, preferred_element_type=jnp.float32
        )
        * 0.125
    )
    allowed = jnp.arange(length, dtype=jnp.int32)[None, :] <= positions[:, None]
    scores = jnp.where(allowed, scores, -jnp.inf)
    new_peak = jnp.max(scores, axis=-1)
    exp_terms = jnp.exp(scores - new_peak[..., None])
    denom_run = jnp.sum(exp_terms, axis=-1)
    running = jnp.einsum(
        "sgrqk,skgd->sgrqd",
        exp_terms.astype(jnp.bfloat16),
        value_heads,
        preferred_element_type=jnp.float32,
    )
    attended_wide = running / denom_run[..., None]
    attended = jnp.transpose(attended_wide, (0, 3, 1, 2, 4)).astype(jnp.bfloat16)
    logsum = new_peak + jnp.log(denom_run)
    attended_rows = attended.reshape(row_count, HEADS * head_size)
    attended_parts = cut(attended_rows, split_count)
    resid2 = resid1 + forward_dot(attended_parts, full_out)
    normal2 = normed(resid2, gain_second).astype(jnp.bfloat16)
    normal2_parts = cut(normal2, split_count)
    gate_act = forward_dot(normal2_parts, full_gate)
    up_act = forward_dot(normal2_parts, full_up)
    gate_sigma = jax.nn.sigmoid(gate_act)
    hidden = (gate_act * gate_sigma * up_act).astype(jnp.bfloat16)
    hidden_parts = cut(hidden, split_count)
    output = (resid2 + forward_dot(hidden_parts, full_down)).astype(jnp.bfloat16)

    grad_rows = grad_output.reshape(row_count, model_width)
    sum_down = scatter_rows(weight_terms(grad_rows, hidden_parts, cycle_size))
    grad_hidden = backward_dot(grad_rows, full_down)
    grad_up = (grad_hidden * gate_act * gate_sigma).astype(jnp.bfloat16)
    grad_gate = (grad_hidden * up_act * gate_sigma * (1.0 + gate_act * (1.0 - gate_sigma))).astype(
        jnp.bfloat16
    )
    grad_norm2 = backward_dot(grad_gate, full_gate) + backward_dot(grad_up, full_up)
    normed_out, pull_second = jax.vjp(normed, resid2, gain_second)
    grad_part2, term_gain2 = pull_second(grad_norm2)
    grad_resid2 = grad_rows.astype(jnp.float32) + grad_part2
    grad_branch = grad_resid2.astype(jnp.bfloat16)
    sum_rest = scatter_rows(
        jnp.concatenate(
            [
                weight_terms(grad_branch, attended_parts, cycle_size),
                weight_terms(grad_gate, normal2_parts, cycle_size),
                weight_terms(grad_up, normal2_parts, cycle_size),
            ],
            axis=2,
        )
    )
    grad_attended = backward_dot(grad_branch, full_out).astype(jnp.bfloat16)
    grad_grouped = grad_attended.reshape(seq_count, block_len, groups, repeat_count, head_size)
    row_delta = jnp.sum(
        jnp.transpose(grad_grouped, (0, 2, 3, 1, 4)).astype(jnp.float32) * attended_wide, axis=-1
    )

    def retrace(step_index, loop_state):
        grad_query_acc, grad_pair_all = loop_state
        key_start = step_index * key_block
        pair = lax.dynamic_slice_in_dim(pair_all, key_start, key_block, 1)
        key_heads = pair[..., :kv_width].reshape(seq_count, key_block, groups, head_size)
        value_heads = pair[..., kv_width:].reshape(seq_count, key_block, groups, head_size)
        scores = (
            jnp.einsum(
                "sqgrd,skgd->sgrqk", query_grouped, key_heads, preferred_element_type=jnp.float32
            )
            * 0.125
        )
        allowed = (key_start + jnp.arange(key_block, dtype=jnp.int32))[None, :] <= positions[
            :, None
        ]
        prob_full = jnp.where(allowed, jnp.exp(jnp.where(allowed, scores, -jnp.inf) - logsum[..., None]), 0.0)
        grad_probs = jnp.einsum(
            "sqgrd,skgd->sgrqk", grad_grouped, value_heads, preferred_element_type=jnp.float32
        )
        grad_scores = (prob_full * (grad_probs - row_delta[..., None]) * 0.125).astype(jnp.bfloat16)
        prob_low = prob_full.astype(jnp.bfloat16)
        value_term = jnp.einsum(
            "sgrqk,sqgrd->skgd", prob_low, grad_grouped, preferred_element_type=jnp.float32
        ).reshape(seq_count, key_block, kv_width)
        key_term = jnp.einsum(
            "sgrqk,sqgrd->skgd", grad_scores, query_grouped, preferred_element_type=jnp.float32
        ).reshape(seq_count, key_block, kv_width)
        grad_query_acc = grad_query_acc + jnp.einsum(
            "sgrqk,skgd->sgrqd", grad_scores, key_heads, preferred_element_type=jnp.float32
        )
        pair_term = jnp.concatenate([key_term, value_term], axis=-1).astype(jnp.bfloat16)
        grad_pair_all = lax.dynamic_update_slice_in_dim(grad_pair_all, pair_term, key_start, 1)
        return (grad_query_acc, grad_pair_all)

    back_state = (
        jnp.zeros((seq_count, groups, repeat_count, block_len, head_size), jnp.float32),
        jnp.zeros((seq_count, length, 2 * kv_width), jnp.bfloat16),
    )
    grad_query_acc, grad_pair_all = lax.fori_loop(0, needed, retrace, back_state)
    grad_pair_own = lax.psum_scatter(
        grad_pair_all, "ctx", scatter_dimension=1, tiled=True
    ).astype(jnp.float32)
    grad_query_rows = jnp.transpose(grad_query_acc, (0, 3, 1, 2, 4)).reshape(
        row_count, HEADS, head_size
    )
    grad_query = (
        unrotate(grad_query_rows, cosine, sine_table)
        .reshape(row_count, HEADS * head_size)
        .astype(jnp.bfloat16)
    )
    grad_keys = (
        unrotate(
            grad_pair_own[..., :kv_width].reshape(row_count, groups, head_size), cosine, sine_table
        )
        .reshape(row_count, kv_width)
        .astype(jnp.bfloat16)
    )
    grad_values = grad_pair_own[..., kv_width:].reshape(row_count, kv_width).astype(jnp.bfloat16)
    grad_norm1 = backward_dot(grad_query, full_query)
    grad_norm1 = grad_norm1 + backward_dot(grad_keys, full_key)
    grad_norm1 = grad_norm1 + backward_dot(grad_values, full_value)
    normed_first, pull_first = jax.vjp(normed, resid1, gain_first)
    grad_part1, term_gain1 = pull_first(grad_norm1)
    grad_input = (
        (grad_resid2 + grad_part1).astype(jnp.bfloat16).reshape(seq_count, block_len, model_width)
    )
    gain_terms = jnp.concatenate(
        [term_gain1.reshape(cycle_size, -1), term_gain2.reshape(cycle_size, -1)], axis=-1
    ).astype(jnp.bfloat16)
    gain_terms = jnp.pad(gain_terms, ((0, 0), (0, part_width - 2 * gain_size)))
    gain_terms = jnp.broadcast_to(
        gain_terms[None, :, None, :], (split_count, cycle_size, 1, part_width)
    )
    sum_first = scatter_rows(
        jnp.concatenate(
            [
                weight_terms(grad_query, normal1_parts, cycle_size),
                weight_terms(grad_keys, normal1_parts, cycle_size),
                weight_terms(grad_values, normal1_parts, cycle_size),
                gain_terms,
            ],
            axis=2,
        )
    )
    gain_sums = sum_first[wide_q + wide_k + wide_v]
    return (
        output.reshape(seq_count, block_len, model_width),
        grad_input,
        sum_first[:wide_q].T,
        sum_first[wide_q : wide_q + wide_k].T,
        sum_first[wide_q + wide_k : wide_q + wide_k + wide_v].T,
        sum_rest[:wide_o].T,
        sum_rest[wide_o : wide_o + wide_g].T,
        sum_rest[wide_o + wide_g : wide_o + wide_g + wide_u].T,
        sum_down.T,
        gain_sums[:gain_size],
        gain_sums[gain_size : 2 * gain_size],
    )


def solution(mesh):
    return jax.shard_map(
        local,
        mesh=mesh,
        in_specs=(
            P("fsdp", "ctx", None),
            P("fsdp", "ctx", None),
            P("fsdp", "ctx"),
            P("fsdp", "ctx"),
            P("fsdp", "ctx"),
            P("fsdp", "ctx"),
            P("fsdp", "ctx"),
            P("fsdp", "ctx"),
            P("fsdp", "ctx"),
            P("ctx"),
            P("ctx"),
        ),
        out_specs=(
            P("fsdp", "ctx", None),
            P("fsdp", "ctx", None),
            P("fsdp", "ctx"),
            P("fsdp", "ctx"),
            P("fsdp", "ctx"),
            P("fsdp", "ctx"),
            P("fsdp", "ctx"),
            P("fsdp", "ctx"),
            P("fsdp", "ctx"),
            P("ctx"),
            P("ctx"),
        ),
        check_vma=False,
    )
```

time: 1190 us -> 917 us (0.77)
  blocking collectives: 332 us -> 0 us
  local copies, waits for them, and re-layouts: 54.1 us -> 161 us
  waiting for transfers between devices: 651 us -> 600 us
  other arithmetic: 18.4 us -> 49.6 us
  starting transfers between devices: 28.3 us -> 0.85 us
    unnamed x3 -> x0, blocking collectives: 210 us -> none
    all_gather x6 -> x0, blocking collectives: 117 us -> none  [the longest x1 26.8 us: local(): lax.all_gather(w_query, 'ctx', axis=1, tiled=True)]
    all_gather x10 -> x4, waiting for transfers between devices: 273 us -> 181 us  [the longest x3 153 us: gather_rows(): gathered = lax.all_gather(packed, BOTH, axis=0, tiled=False)]
    another operation x2 -> x31, local copies, waits for them, and re-layouts: 3.69 us -> 75.5 us  [the longest x21 55.5 us: take(): return [part.reshape(-1, part.shape[-1]) for part in piece]]
    reduce_scatter x7 -> x3, waiting for transfers between devices: 319 us -> 363 us  [scatter_rows(): lax.psum_scatter(merged, BOTH, scatter_dimension=0, tiled=True)[0]]
    unnamed x11 -> x1, starting transfers between devices: 27.2 us -> 0.57 us
    unnamed x106 -> x123, local copies, waits for them, and re-layouts: 33.8 us -> 56.4 us
    convert_element_type x0 -> x6, local copies, waits for them, and re-layouts: none -> 17.8 us  [the longest x4 16.3 us: weight_terms(): terms = [lax.dot_general(grads, piece, (((0,), (0,)), ((), ())), preferre...]
  transfers between devices with their start and end apart: 28 -> 8, of which waited for: 15 -> 8; matrix products, arithmetic and copies ran while one was open for 18% -> 21% of each run, Pallas kernels for 0% -> 0%
where the time goes in v1:
time: 917 us; the launch traced here: 910 us
  waiting for transfers between devices  600 us (65%)
  local copies, waits for them, and re-layouts  161 us (18%)
  matrix products  82.2 us (9%)
  other arithmetic  49.6 us (5%)
  between operations  15.3 us (2%)
    reduce_scatter x3, waiting for transfers between devices, scatter_rows(): lax.psum_scatter(merged, BOTH, scatter_dimension=0, tiled=True)[0]  363 us
    all_gather x3, waiting for transfers between devices, gather_rows(): gathered = lax.all_gather(packed, BOTH, axis=0, tiled=False)  153 us
    unnamed x9, waiting for transfers between devices  56.6 us
    unnamed x123, local copies, waits for them, and re-layouts  56.4 us
    another operation x21, local copies, waits for them, and re-layouts, take(): return [part.reshape(-1, part.shape[-1]) for part in piece]  55.5 us
    all_gather x1, waiting for transfers between devices, local(): lax.all_gather(jnp.concatenate([key_rows, value_rows], axis=-1), 'ctx', a...  27.7 us
    dot_general x14, matrix products, weight_terms(): lax.dot_general(grads, piece, (((0,), (0,)), ((), ())), preferred_element...  24.6 us
    dot_general x14, matrix products, forward_dot(): lax.dot_general(piece, half, (((1,), (1,)), ((), ())), preferred_element_...  21.6 us
  transfers between devices with their start and end apart: 8, of which 8 were waited for; matrix products, arithmetic and copies ran while one was open for 21% of the time, Pallas kernels for 0%

profile of v1, /device:TPU:0, one launch (start us, length us, event | category | flops | bytes accessed | tf_op | source)
XLA Modules:
  0.0 909.7 jit_solution(12347333619238508726)
XLA Ops:
  13.3 60.9 %all-gather.13.cloned.1.call-done = bf16[32,101,480]{2,1,0:T(8,128)(2,1)} async-done(((bf16[1,101,480]{2,1,0:T(8,128)(2,1)}), bf16[32,101,480]{2,1,0:T(8,128)(2,1)}) %all-gather.13.cloned.1.call-update) | async-done | bytes 3102736 | tf_op jit(solution)/shard_map/all_gather | solution.py:87
  115.7 25.2 %all-gather.17.cloned.1.call-done = bf16[32,60,1280]{2,1,0:T(8,128)(2,1)} async-done(((bf16[1,60,1280]{2,1,0:T(8,128)(2,1)}), bf16[32,60,1280]{2,1,0:T(8,128)(2,1)}) %all-gather.17.cloned.1.call-update) | async-done | bytes 4915216 | tf_op jit(solution)/shard_map/all_gather | solution.py:87
  140.9 5.5 fusion.138
  149.1 4.8 reshape.478
  157.3 27.7 %all-gather.11.cloned.1.call-done = bf16[1,2048,640]{1,2,0:T(8,128)(2,1)} async-done(((bf16[1,128,640]{1,2,0:T(8,128)(2,1)}), bf16[1,2048,640]{1,2,0:T(8,128)(2,1)}) %all-gather.11.cloned.1.call-update) | async-done | bytes 2621456 | tf_op jit(solution)/shard_map/all_gather | solution.py:160
  186.9 6.8 fusion.45
  193.7 8.9 fusion.43
  202.6 8.3 fusion.142
  210.9 67.0 %all-gather.15.cloned.1.call-done = bf16[32,380,480]{1,2,0:T(8,128)(2,1)} async-done(((bf16[1,380,480]{1,2,0:T(8,128)(2,1)}), bf16[32,380,480]{1,2,0:T(8,128)(2,1)}) %all-gather.15.cloned.1.call-update) | async-done | bytes 11673616 | tf_op jit(solution)/shard_map/all_gather | solution.py:87
  277.9 3.7 fusion.137
  281.6 16.0 %fusion.136 = (bf16[1,16,160,480]{2,3,1,0:T(8,128)(2,1)}, bf16[1,16,160,480]{2,3,1,0:T(8,128)(2,1)}, bf16[1,16,160,480]{2,3,1,0:T(8,128)(2,1)}, bf16[1,16,160,480]{2,3,1,0:T(8,128)(2,1)}) fusion(bf16[2,16,380,480]{2,3,1,0:T(8,128)(2,1)} %bitcast.375), kind=kLoop, calls=%fused_computation.214 | loop fusion | bytes 19660800 | tf_op jit(solution)/shard_map/unstack | solution.py:93
  306.7 5.8 copy.130
  312.5 5.1 copy.132
  317.8 4.6 fusion.105
  324.6 5.0 copy.133
  329.6 6.0 copy.131
  350.7 7.0 while.13
  357.8 11.7 %copy.125 = bf16[1,2048,640]{2,0,1:T(2,128)(2,1)} copy(bf16[1,2048,640]{1,2,0:T(8,128)(2,1)} %get-tuple-element.66) | data formatting | bytes 5242880
  369.5 4.5 copy.135
  377.4 4.2 stack_reshape.54
  383.8 4.1 stack_reshape.55
  387.9 5.3 pad_maximum_fusion
  402.2 55.8 %reduce-scatter.13.cloned.1.call-done = bf16[128,640]{1,0:T(8,128)(2,1)} async-done(((bf16[2048,640]{1,0:T(8,128)(2,1)}), bf16[128,640]{1,0:T(8,128)(2,1)}) %reduce-scatter.13.cloned.1.call-update) | async-done | bytes 163856
  471.7 3.7 pad_maximum_fusion.1
  491.4 3.5 convolution_convert_fusion.2
  494.9 4.4 copy.112
  502.7 4.4 copy.113
  510.5 4.4 copy.114
  514.9 11.6 %maximum_maximum_fusion = bf16[2,16,380,480]{3,2,1,0:T(8,128)(2,1)} fusion(bf16[1,16,160,480]{3,2,1,0:T(8,128)(2,1)} %bitcast.394, bf16[1,16,160,480]{3,2,1,0:T(8,128)(2,1)} %bitcast.393, bf16[1,16,160,480]{3,2,1,0:T(8,128)(2,1)} %bitcast.392, bf16[1,16,160,480]{3,2,1,0:T(8,128)(2,1)S(1)} %bitcast.389, bf16[1,16,60,480]{3,2,1,0:T(8,128)(2,1)} %stack_reshape.49, ...), kind=kLoop, calls=%fused_computation.41 | loop fusion | flops 70041600 | bytes 23347200 | tf_op jit(solution)/shard_map/concatenate | solution.py:212
  532.8 71.2 %reduce-scatter.11.cloned.1.call-done = bf16[1,60,1280]{2,1,0:T(8,128)(2,1)} async-done(((bf16[32,60,1280]{2,1,0:T(8,128)(2,1)}), bf16[1,60,1280]{2,1,0:T(8,128)(2,1)}) %reduce-scatter.11.cloned.1.call-update) | async-done | bytes 153616 | tf_op jit(solution)/shard_map/reduce_scatter | solution.py:98
  605.6 137.3 %reduce-scatter.7.cloned.1.call-done = bf16[1,101,480]{2,1,0:T(8,128)(2,1)} async-done(((bf16[32,101,480]{2,1,0:T(8,128)(2,1)}), bf16[1,101,480]{2,1,0:T(8,128)(2,1)}) %reduce-scatter.7.cloned.1.call-update) | async-done | bytes 96976 | tf_op jit(solution)/shard_map/reduce_scatter | solution.py:98
  745.8 154.2 %reduce-scatter.9.cloned.1.call-done = bf16[1,380,480]{2,1,0:T(8,128)(2,1)} async-done(((bf16[32,380,480]{2,1,0:T(8,128)(2,1)}), bf16[1,380,480]{2,1,0:T(8,128)(2,1)}) %reduce-scatter.9.cloned.1.call-update) | async-done | bytes 364816 | tf_op jit(solution)/shard_map/reduce_scatter | solution.py:98
  (262 shorter events, 152.6 us)
Async XLA Ops:
  7.2 67.1 %all-gather.13.cloned.1.call-start = ((), (), s32[]{:S(2)}) async-start(), calls=%async_computation.8 | async-start | bytes 3514368 | tf_op jit(solution)/shard_map/all_gather | solution.py:87
  9.5 131.4 %all-gather.17.cloned.1.call-start = ((), (), s32[]{:S(2)}) async-start(), calls=%async_computation.10 | async-start | bytes 5406720 | tf_op jit(solution)/shard_map/all_gather | solution.py:87
  10.3 174.7 %all-gather.11.cloned.1.call-start = ((), (), s32[]{:S(2)}) async-start(), calls=%async_computation.4 | async-start | bytes 2785280 | tf_op jit(solution)/shard_map/all_gather | solution.py:160
  93.7 5.7 copy-start.36
  94.9 20.3 %copy-start.7 = (bf16[128,960]{0,1:T(8,128)(2,1)}, bf16[128,960]{0,1:T(8,128)(2,1)S(1)}, u32[]{:S(2)}) copy-start(bf16[128,960]{0,1:T(8,128)(2,1)S(1)} %fusion.66) | copy-start | bytes 737284
  100.4 177.5 %all-gather.15.cloned.1.call-start = ((), (), s32[]{:S(2)}) async-start(), calls=%async_computation.9 | async-start | bytes 12165120 | tf_op jit(solution)/shard_map/all_gather | solution.py:87
  107.8 350.2 %reduce-scatter.13.cloned.1.call-start = ((), (), s32[]{:S(2)}) async-start(), calls=%async_computation.11 | async-start | bytes 2785280
  110.9 3.1 copy-start.51
  111.4 3.8 copy-start.16
  114.0 32.4 %copy-start.18 = (bf16[960,480]{1,0:T(8,128)(2,1)}, bf16[960,480]{1,0:T(8,128)(2,1)S(1)}, u32[]{:S(2)}) copy-start(bf16[960,480]{1,0:T(8,128)(2,1)S(1)} %reshape_unstack.47) | copy-start | bytes 2764804
  149.1 6.2 copy-start.3
  149.1 4.8 copy-start.13
  157.3 29.6 %copy-start.35 = (pred[128,2048]{0,1:T(8,128)(4,1)S(1)}, pred[128,2048]{0,1:T(8,128)(4,1)}, u32[]{:S(2)}) copy-start(pred[128,2048]{0,1:T(8,128)(4,1)} %iota_compare_fusion) | copy-start | bytes 786436
  210.9 95.3 %copy-start.42 = (bf16[1,5,3,128,64]{3,4,2,1,0:T(8,128)(2,1)}, bf16[1,5,3,128,64]{3,4,2,1,0:T(8,128)(2,1)S(1)}, u32[]{:S(2)}) copy-start(bf16[1,5,3,128,64]{3,4,2,1,0:T(8,128)(2,1)S(1)} %get-tuple-element.160) | copy-start | bytes 737284
  300.9 5.3 copy-start.20
  301.0 5.3 copy-start.25
  305.8 6.7 copy-start.22
  312.5 5.1 copy-start.49
  317.6 7.0 copy-start
  317.8 6.8 copy-start.28
  338.4 3.3 copy-start.2
  341.8 4.0 copy-start.10
  373.9 230.0 %reduce-scatter.11.cloned.1.call-start = ((), (), s32[]{:S(2)}) async-start(), calls=%async_computation.7 | async-start | bytes 5406720 | tf_op jit(solution)/shard_map/reduce_scatter | solution.py:98
  393.2 349.7 %reduce-scatter.7.cloned.1.call-start = ((), (), s32[]{:S(2)}) async-start(), calls=%async_computation.5 | async-start | bytes 3514368 | tf_op jit(solution)/shard_map/reduce_scatter | solution.py:98
  394.6 5.1 copy-start.17
  395.9 5.1 copy-start.19
  461.6 7.7 copy-start.26
  461.6 7.7 copy-start.50
  461.6 7.7 copy-start.52
  463.8 7.9 copy-start.33
  463.8 7.9 copy-start.34
  475.4 424.5 %reduce-scatter.9.cloned.1.call-start = ((), (), s32[]{:S(2)}) async-start(), calls=%async_computation.6 | async-start | bytes 12976128 | tf_op jit(solution)/shard_map/reduce_scatter | solution.py:98
  (31 other events, 49.9 us)
Sparse Core Ops, SparseCore 0:
  11.4 62.7 all-gather.12
  77.1 63.8 all-gather.16
  143.1 41.8 all-gather.10
  187.7 90.0 all-gather.14
  374.1 83.9 reduce-scatter.12
  460.2 143.7 reduce-scatter.10
  606.3 136.6 reduce-scatter.6
  748.9 150.9 reduce-scatter.8
